TPU v7x, 32 devices: a whole 2x2x4 slice. The times are simulated.
32 devices in a mesh: tm: 16 (over z, x, core), space: 2 (over y).
Axes of the slice: x: 2, y: 2, z: 4, core: 2. Of those that a mesh axis runs over, the one named last changes fastest.
Arguments:
- conv_input: bfloat16 [16, 12, 40, 256], P('tm', None, 'space'), may hold values from -6 to 6
- conv_out: bfloat16 [16, 12, 40, 256], P('tm', None, 'space'), may hold values from -20 to 20
- kernel: bfloat16 [3, 3, 3, 256, 256], replicated, may hold values from -0.078125 to 0.078125
- gain: float32 [256], replicated, may hold values from 0.25 to 1.75
- bias: float32 [256], replicated, may hold values from -4 to 4
- cotangent: bfloat16 [16, 12, 40, 256], P('tm', None, 'space'), may hold values from -7 to 7
Outputs:
- grad_input: bfloat16 [16, 12, 40, 256], P('tm', None, 'space')
- grad_kernel: float32 [3, 3, 3, 256, 256], P(None, None, None, None, 'space')
- grad_gain: float32 [256], replicated
- grad_bias: float32 [256], replicated
All inputs are finite; a program needn't handle non-finite values.
Results may differ from a plain program's by a relative error of at most 0.0075.
Values may be sent and summed in bfloat16 or wider, within the bound.
A program may use at most 64 MiB of HBM per device.

v0:
```python
import jax
import jax.numpy as jnp
from jax import lax
from jax.sharding import PartitionSpec as P

GROUPS = 32
epsilon = 1e-06


def shifted_2(x, axis, by):
    size = lax.axis_size(axis)
    pairs = [(i, i + by) for i in range(size) if 0 <= i + by < size]
    return lax.ppermute(x, axis, pairs)


def extended_2(cells, sides, width):
    for axis, dim in sides:
        count = lax.axis_size(axis)
        ends = count - 1
        head = lax.slice_in_dim(cells, 0, width, axis=dim)
        tail = lax.slice_in_dim(cells, cells.shape[dim] - width, cells.shape[dim], axis=dim)
        cells = jnp.concatenate(
            [
                lax.ppermute(tail, axis, [(i, (i + 1) % count) for i in range(ends)]),
                cells,
                lax.ppermute(head, axis, [((i + 1) % count, i) for i in range(ends)]),
            ],
            axis=dim,
        )
    return cells


def frame_shift(block, step):
    return shifted_2(block, "tm", step)


def return_shift(block, step):
    return shifted_2(block.astype(jnp.bfloat16), "tm", step).astype(block.dtype)


def shards(conv_input, conv_out, kernel, gain, bias, cotangent):
    frames, rows, cols, chans = conv_out.shape
    width = chans // GROUPS
    grouped = conv_out.astype(jnp.float32).reshape(frames, rows, cols, GROUPS, width)
    total, square = lax.psum(
        (jnp.sum(grouped, axis=(0, 1, 2, 4)), jnp.sum(grouped * grouped, axis=(0, 1, 2, 4))),
        ("tm", "space"),
    )
    count = frames * rows * cols * width * lax.axis_size("tm") * lax.axis_size("space")
    mean = total / count
    inv_std = lax.rsqrt(square / count - mean * mean + epsilon)
    normed_grouped = (grouped - mean[:, None]) * inv_std[:, None]
    normed = normed_grouped.reshape(frames, rows, cols, chans)
    shifted = normed * gain + bias
    sigma = jax.nn.sigmoid(shifted)
    grad_shift = cotangent.astype(jnp.float32) * sigma * (1.0 + shifted * (1.0 - sigma))
    grad_grouped = (grad_shift * gain).reshape(frames, rows, cols, GROUPS, width)
    chan_bias, chan_gain = lax.psum(
        (jnp.sum(grad_shift, axis=(0, 1, 2)), jnp.sum(grad_shift * normed, axis=(0, 1, 2))),
        ("tm", "space"),
    )
    plain = jnp.sum((chan_bias * gain).reshape(GROUPS, width), axis=1)
    product = jnp.sum((chan_gain * gain).reshape(GROUPS, width), axis=1)
    grad_conv = inv_std[:, None] * (
        grad_grouped - plain[:, None] / count - normed_grouped * product[:, None] / count
    )
    grad_conv = grad_conv.reshape(frames, rows, cols, chans).astype(jnp.bfloat16)
    reach = 2
    earlier = [frame_shift(conv_input, step) for step in range(reach, 0, -1)]
    extended = jnp.concatenate(earlier + [conv_input], axis=0)
    whole_inputs = lax.all_gather(extended, "space", axis=2, tiled=True)
    channel_grads = lax.all_to_all(grad_conv, "space", split_axis=3, concat_axis=2, tiled=True)
    padded_inputs = jnp.pad(whole_inputs, ((0, 0), (1, 1), (1, 1), (0, 0)))
    wide = channel_grads.shape[2]
    contract = (((0, 1, 2), (0, 1, 2)), ((), ()))
    taps = []
    for tap_t in range(3):
        for tap_h in range(3):
            for tap_w in range(3):
                source = padded_inputs[
                    tap_t : tap_t + frames, tap_h : tap_h + rows, tap_w : tap_w + wide
                ]
                taps.append(
                    lax.dot_general(
                        source, channel_grads, contract, preferred_element_type=jnp.float32
                    )
                )
    local_kernel = jnp.stack(taps).reshape(3, 3, 3, chans, channel_grads.shape[3])
    rimmed = extended_2(grad_conv, (("space", 2),), 1)
    padded = jnp.pad(rimmed, ((0, 0), (1, 1), (0, 0), (0, 0)))
    transpose = (((3,), (1,)), ((), ()))
    partial_sums = jnp.zeros((frames + 2, rows, cols, chans), jnp.float32)
    for tap_t in range(3):
        section = jnp.zeros((frames, rows, cols, chans), jnp.float32)
        for tap_h in range(3):
            for tap_w in range(3):
                window = padded[:, 2 - tap_h : 2 - tap_h + rows, 2 - tap_w : 2 - tap_w + cols]
                section = section + lax.dot_general(
                    window,
                    kernel[tap_t, tap_h, tap_w],
                    transpose,
                    preferred_element_type=jnp.float32,
                )
        partial_sums = partial_sums.at[tap_t : tap_t + frames].add(section)
    local_part = partial_sums[2:]
    local_part = (
        local_part + return_shift(partial_sums[0:1], -2) + return_shift(partial_sums[1:2], -1)
    )
    grad_input = local_part.astype(jnp.bfloat16)
    grad_kernel = lax.psum(local_kernel, "tm")
    return (grad_input, grad_kernel, chan_gain, chan_bias)


def solution(mesh):
    return jax.shard_map(
        shards,
        mesh=mesh,
        in_specs=(
            P("tm", None, "space", None),
            P("tm", None, "space", None),
            P(),
            P(),
            P(),
            P("tm", None, "space", None),
        ),
        out_specs=(P("tm", None, "space", None), P(None, None, None, None, "space"), P(), P()),
        check_vma=False,
    )
```

profile of v0, /device:TPU:0, one launch (start us, length us, event | category | flops | bytes accessed | tf_op | source)
XLA Modules:
  0.0 271.4 jit_solution(3972550199970189502)
XLA Ops:
  7.2 0.9 copy.12
  8.1 2.4 collective-permute-start.5
  10.5 1.0 fusion.39
  11.9 4.4 %collective-permute-start.4 = (bf16[1,12,20,256]{3,1,0,2:T(8,128)(2,1)S(1)}, bf16[1,12,20,256]{3,1,0,2:T(8,128)(2,1)S(1)}, u32[]{:S(2)}, u32[]{:S(2)}) collective-permute-start(bf16[1,12,20,256]{3,1,0,2:T(8,128)(2,1)S(1)} %copy.12), channel_id=1, source_target_pairs={{0,4},{2,6},{4,8},{6,10},{8,12},{10,14},{12,16},{14,18},{16,20},{1... | collective-permute-start | bytes 368648 | tf_op jit(solution)/shard_map/ppermute | solution.py:13
  16.3 40.7 %all-reduce.3 = (f32[32]{0:T(128)S(1)}, f32[32]{0:T(128)S(1)}) all-reduce(f32[32]{0:T(128)S(1)} %reduce_sum.73, f32[32]{0:T(128)S(1)} %reduce_sum.70), channel_id=1, replica_groups=mesh['tm'=16,'space'=2] {'tm','space'}, use_global_device_ids=true, to_apply=%region_5.0 | all-reduce | flops 64 | bytes 512 | tf_op jit(solution)/shard_map/psum | solution.py:45
  57.4 1.2 fusion.214
  58.6 39.8 %all-reduce.2 = (f32[256]{0:T(256)S(1)}, f32[256]{0:T(256)S(1)}) all-reduce(f32[256]{0:T(256)S(1)} %get-tuple-element.41, f32[256]{0:T(256)S(1)} %get-tuple-element.40), channel_id=1, replica_groups=mesh['tm'=16,'space'=2] {'tm','space'}, use_global_device_ids=true, to_apply=%region_10.11 | all-reduce | flops 512 | bytes 4096 | tf_op jit(solution)/shard_map/psum | solution.py:58
  98.4 0.7 fusion.217
  99.8 1.0 fusion.56
  100.9 4.2 %collective-permute-start = (bf16[1,12,1,256]{3,2,1,0:T(2,128)(2,1)S(1)}, bf16[1,12,1,256]{3,2,1,0:T(2,128)(2,1)S(1)}, u32[]{:S(2)}, u32[]{:S(2)}) collective-permute-start(bf16[1,12,1,256]{3,2,1,0:T(2,128)(2,1)S(1)} %get-tuple-element.49), channel_id=1, source_target_pairs={{0,1},{2,3},{4,5},{6,7},{8,9},{10,11},{12,13},{14,15},{16,17},{18,... | collective-permute-start | bytes 18440 | tf_op jit(solution)/shard_map/ppermute | solution.py:24
  105.1 1.3 collective-permute-start.1
  106.4 1.0 copy.16
  107.4 1.8 reshape.522
  109.1 3.9 %all-to-all-start = ((bf16[2,2,15360]{2,1,0:T(2,128)(2,1)}), bf16[2,2,15360]{2,1,0:T(2,128)(2,1)S(1)}, u32[]{:S(2)}, u32[]{:S(2)}) async-start(bf16[2,2,15360]{2,1,0:T(2,128)(2,1)} %reshape.522), calls=%async_computation | async-start | bytes 245760 | tf_op jit(solution)/shard_map/all_to_all | solution.py:72
  113.1 1.3 fusion.114
  114.3 1.1 fusion.112
  115.5 1.1 fusion.116
  116.7 1.1 fusion.131
  117.9 1.1 fusion.120
  119.0 1.1 fusion.138
  121.6 0.2 fusion.3
  122.5 1.3 collective-permute-start.2
  124.8 1.3 collective-permute-start.3
  126.1 1.1 reshape.523
  127.3 0.8 copy.17
  128.2 14.7 %all_gather.3 = bf16[3,12,40,256]{3,1,0,2:T(8,128)(2,1)S(1)} all-gather(bf16[3,12,20,256]{3,1,0,2:T(8,128)(2,1)S(1)} %pad_maximum_fusion), channel_id=1, replica_groups=mesh['tm'=16,'space'=2] {'space'}, dimensions={2}, use_global_device_ids=true | all-gather | bytes 1105920 | tf_op jit(solution)/shard_map/all_gather | solution.py:71
  143.1 0.3 fusion.37
  143.3 0.3 fusion.36
  143.6 0.3 fusion.35
  143.8 0.3 fusion.34
  144.1 0.3 fusion.33
  144.4 0.3 fusion.32
  144.6 0.3 fusion.31
  144.9 0.3 fusion.30
  145.2 0.3 fusion.29
  145.4 0.3 fusion.28
  145.7 0.3 fusion.27
  146.0 0.3 fusion.26
  146.2 0.3 fusion.25
  146.5 0.3 fusion.24
  146.8 0.3 fusion.23
  147.0 0.3 fusion.22
  147.3 0.3 fusion.21
  147.6 0.3 fusion.20
  147.8 0.3 fusion.19
  148.1 0.3 fusion.18
  148.4 0.3 fusion.17
  148.6 0.3 fusion.16
  148.9 0.3 fusion.15
  149.2 0.3 fusion.14
  149.4 0.3 fusion.13
  149.7 0.3 fusion.12
  150.0 0.3 fusion.11
  150.2 1.8 copy-done
  152.0 1.1 fusion.149
  153.2 1.1 convolution_add_fusion.17
  154.3 1.1 convolution_add_fusion.16
  155.5 1.1 fusion.6
  156.6 1.1 fusion.5
  157.8 1.1 convolution_add_fusion.13
  158.9 1.2 fusion.4
  160.1 0.7 add_convert_fusion
  160.8 99.6 %all-reduce.6.cloned.1.call-done = f32[3,3,3,256,128]{4,3,2,1,0:T(8,128)} async-done(((f32[3,3,3,256,128]{4,3,2,1,0:T(8,128)}), f32[3,3,3,256,128]{4,3,2,1,0:T(8,128)}) %all-reduce.6.cloned.1.call-update) | async-done | bytes 3538960 | tf_op jit(solution)/shard_map/psum | solution.py:110
  260.4 4.2 %copy.48 = f32[3,3,3,256,128]{4,3,2,1,0:T(8,128)} copy(f32[3,3,3,256,128]{4,3,2,1,0:T(8,128)} %all-reduce.6.cloned.1.call-done) | data formatting | bytes 7077888
  (52 shorter events, 5.0 us)
Async XLA Ops:
  8.1 120.0 %collective-permute-start.5 = (bf16[1,12,20,256]{3,1,0,2:T(8,128)(2,1)S(1)}, bf16[1,12,20,256]{3,1,0,2:T(8,128)(2,1)S(1)}, u32[]{:S(2)}, u32[]{:S(2)}) collective-permute-start(bf16[1,12,20,256]{3,1,0,2:T(8,128)(2,1)S(1)} %copy.12), channel_id=1, source_target_pairs={{0,2},{2,4},{4,6},{6,8},{8,10},{10,12},{12,14},{14,16},{16,18},{18... | collective-permute-start | bytes 368648 | tf_op jit(solution)/shard_map/ppermute | solution.py:13
  11.9 116.2 %collective-permute-start.4 = (bf16[1,12,20,256]{3,1,0,2:T(8,128)(2,1)S(1)}, bf16[1,12,20,256]{3,1,0,2:T(8,128)(2,1)S(1)}, u32[]{:S(2)}, u32[]{:S(2)}) collective-permute-start(bf16[1,12,20,256]{3,1,0,2:T(8,128)(2,1)S(1)} %copy.12), channel_id=1, source_target_pairs={{0,4},{2,6},{4,8},{6,10},{8,12},{10,14},{12,16},{14,18},{16,20},{1... | collective-permute-start | bytes 368648 | tf_op jit(solution)/shard_map/ppermute | solution.py:13
  98.4 21.8 %copy-start.2 = (f32[256]{0:T(256)}, f32[256]{0:T(256)S(1)}, u32[]{:S(2)}) copy-start(f32[256]{0:T(256)S(1)} %get-tuple-element.57) | copy-start | bytes 3076
  98.4 21.8 %copy-start.3 = (f32[256]{0:T(256)}, f32[256]{0:T(256)S(1)}, u32[]{:S(2)}) copy-start(f32[256]{0:T(256)S(1)} %get-tuple-element.58) | copy-start | bytes 3076
  100.9 15.7 %collective-permute-start = (bf16[1,12,1,256]{3,2,1,0:T(2,128)(2,1)S(1)}, bf16[1,12,1,256]{3,2,1,0:T(2,128)(2,1)S(1)}, u32[]{:S(2)}, u32[]{:S(2)}) collective-permute-start(bf16[1,12,1,256]{3,2,1,0:T(2,128)(2,1)S(1)} %get-tuple-element.49), channel_id=1, source_target_pairs={{0,1},{2,3},{4,5},{6,7},{8,9},{10,11},{12,13},{14,15},{16,17},{18,... | collective-permute-start | bytes 18440 | tf_op jit(solution)/shard_map/ppermute | solution.py:24
  105.1 11.6 %collective-permute-start.1 = (bf16[1,12,1,256]{3,2,1,0:T(2,128)(2,1)S(1)}, bf16[1,12,1,256]{3,2,1,0:T(2,128)(2,1)S(1)}, u32[]{:S(2)}, u32[]{:S(2)}) collective-permute-start(bf16[1,12,1,256]{3,2,1,0:T(2,128)(2,1)S(1)} %get-tuple-element.50), channel_id=1, source_target_pairs={{1,0},{3,2},{5,4},{7,6},{9,8},{11,10},{13,12},{15,14},{17,16},{19,... | collective-permute-start | bytes 18440 | tf_op jit(solution)/shard_map/ppermute | solution.py:26
  109.1 16.9 %all-to-all-start = ((bf16[2,2,15360]{2,1,0:T(2,128)(2,1)}), bf16[2,2,15360]{2,1,0:T(2,128)(2,1)S(1)}, u32[]{:S(2)}, u32[]{:S(2)}) async-start(bf16[2,2,15360]{2,1,0:T(2,128)(2,1)} %reshape.522), calls=%async_computation | async-start | bytes 245760 | tf_op jit(solution)/shard_map/all_to_all | solution.py:72
  113.1 147.4 %all-reduce.6.cloned.1.call-start = ((), (), s32[]{:S(2)}) async-start(), calls=%async_computation.1 | async-start | bytes 7077888 | tf_op jit(solution)/shard_map/psum | solution.py:110
  113.1 7.1 %copy-start.1 = (bf16[3,3,3,256,256]{4,3,2,1,0:T(8,128)(2,1)S(1)}, bf16[3,3,3,256,256]{4,3,2,1,0:T(8,128)(2,1)}, u32[]{:S(2)}) copy-start(bf16[3,3,3,256,256]{4,3,2,1,0:T(8,128)(2,1)} %param.14) | copy-start | bytes 10616836
  122.5 37.6 %collective-permute-start.2 = (bf16[1,12,20,256]{3,2,1,0:T(8,128)(2,1)S(1)}, bf16[1,12,20,256]{3,2,1,0:T(8,128)(2,1)S(1)}, u32[]{:S(2)}, u32[]{:S(2)}) collective-permute-start(bf16[1,12,20,256]{3,2,1,0:T(8,128)(2,1)S(1)} %fusion.10), channel_id=1, source_target_pairs={{4,0},{6,2},{8,4},{10,6},{12,8},{14,10},{16,12},{18,14},{20,16},{2... | collective-permute-start | bytes 368648 | tf_op jit(solution)/shard_map/ppermute | solution.py:13
  124.8 35.3 %collective-permute-start.3 = (bf16[1,12,20,256]{3,2,1,0:T(8,128)(2,1)S(1)}, bf16[1,12,20,256]{3,2,1,0:T(8,128)(2,1)S(1)}, u32[]{:S(2)}, u32[]{:S(2)}) collective-permute-start(bf16[1,12,20,256]{3,2,1,0:T(8,128)(2,1)S(1)} %fusion.9), channel_id=1, source_target_pairs={{2,0},{4,2},{6,4},{8,6},{10,8},{12,10},{14,12},{16,14},{18,16},{20... | collective-permute-start | bytes 368648 | tf_op jit(solution)/shard_map/ppermute | solution.py:13
  150.2 1.8 copy-start
Sparse Core Ops, SparseCore 0:
  152.2 108.2 all-reduce.5
where the time goes:
time: 272 us; the launch traced here: 271 us
  waiting for transfers between devices  99.6 us (37%)
  blocking collectives  95.2 us (35%)
  matrix products  25.2 us (9%)
  starting transfers between devices  18.8 us (7%)
  between operations  14.5 us (5%)
  local copies, waits for them, and re-layouts  12.9 us (5%)
  other arithmetic  5.27 us (2%)
    psum x1, waiting for transfers between devices, shards(): grad_kernel = lax.psum(local_kernel, 'tm')  99.6 us
    psum x1, blocking collectives, shards(): lax.psum((jnp.sum(grouped, axis=(0, 1, 2, 4)), jnp.sum(grouped * grouped,...  40.7 us
    psum x1, blocking collectives, shards(): lax.psum((jnp.sum(grad_shift, axis=(0, 1, 2)), jnp.sum(grad_shift * norme...  39.8 us
    dot_general x27, matrix products, shards(): lax.dot_general(window, kernel[tap_t, tap_h, tap_w], transpose, preferred...  18.1 us
    all_gather x1, blocking collectives, shards(): whole_inputs = lax.all_gather(extended, 'space', axis=2, tiled=True)  14.7 us
    unnamed x12, local copies, waits for them, and re-layouts  9.84 us
    ppermute x4, starting transfers between devices, shifted_2(): return lax.ppermute(x, axis, pairs)  9.39 us
    dot_general x27, matrix products, shards(): lax.dot_general(source, channel_grads, contract, preferred_element_type=j...  7.09 us
  transfers between devices with their start and end apart: 8, of which 1 were waited for; matrix products, arithmetic and copies ran while one was open for 13% of the time, Pallas kernels for 0%

commit v1 on v0

--- a/solution.py
+++ b/solution.py
@@ -107,7 +107,11 @@
         local_part + return_shift(partial_sums[0:1], -2) + return_shift(partial_sums[1:2], -1)
     )
     grad_input = local_part.astype(jnp.bfloat16)
-    grad_kernel = lax.psum(local_kernel, "tm")
+    grad_kernel = local_kernel
+    for hop in (1, 2, 4, 8):
+        grad_kernel = grad_kernel + lax.ppermute(
+            grad_kernel, "tm", [(dev, dev ^ hop) for dev in range(16)]
+        )
     return (grad_input, grad_kernel, chan_gain, chan_bias)
 
 

time: 272 us -> 448 us (1.65)
  waiting for transfers between devices: 99.6 us -> 299 us
  between operations: 14.5 us -> 1.12 us
  matrix products: 25.2 us -> 13.3 us
  local copies, waits for them, and re-layouts: 12.9 us -> 6.25 us
    ppermute x0 -> x4, waiting for transfers between devices: none -> 294 us  [shards(): lax.ppermute(grad_kernel, 'tm', [(dev, dev ^ hop) for dev in range(16)])]
    psum x1 -> x0, waiting for transfers between devices: 99.6 us -> none  [shards(): grad_kernel = lax.psum(local_kernel, 'tm')]
    dot_general x27, matrix products: 18.1 us -> 6.2 us  [shards(): lax.dot_general(window, kernel[tap_t, tap_h, tap_w], transpose, preferred...]
    all_to_all x0 -> x1, blocking collectives: none -> 7.76 us  [shards(): lax.all_to_all(grad_conv, 'space', split_axis=3, concat_axis=2, tiled=True)]
    unnamed x12 -> x9, local copies, waits for them, and re-layouts: 9.84 us -> 3.22 us
    ppermute x0 -> x4, starting transfers between devices: none -> 5.23 us  [shards(): lax.ppermute(grad_kernel, 'tm', [(dev, dev ^ hop) for dev in range(16)])]
  transfers between devices with their start and end apart: 8 -> 10, of which waited for: 1 -> 6; matrix products, arithmetic and copies ran while one was open for 13% -> 4% of each run, Pallas kernels for 0% -> 0%
where the time goes in v1:
time: 448 us; the launch traced here: 446 us
  waiting for transfers between devices  299 us (67%)
  blocking collectives  99.1 us (22%)
  starting transfers between devices  18.1 us (4%)
  matrix products  13.3 us (3%)
  other arithmetic  8.95 us (2%)
  local copies, waits for them, and re-layouts  6.25 us (1%)
    ppermute x4, waiting for transfers between devices, shards(): lax.ppermute(grad_kernel, 'tm', [(dev, dev ^ hop) for dev in range(16)])  294 us
    psum x1, blocking collectives, shards(): lax.psum((jnp.sum(grouped, axis=(0, 1, 2, 4)), jnp.sum(grouped * grouped,...  40.7 us
    psum x1, blocking collectives, shards(): lax.psum((jnp.sum(grad_shift, axis=(0, 1, 2)), jnp.sum(grad_shift * norme...  39.8 us
    all_gather x1, blocking collectives, shards(): whole_inputs = lax.all_gather(extended, 'space', axis=2, tiled=True)  10.9 us
    ppermute x4, starting transfers between devices, shifted_2(): return lax.ppermute(x, axis, pairs)  9.39 us
  transfers between devices with their start and end apart: 10, of which 6 were waited for; matrix products, arithmetic and copies ran while one was open for 4% of the time, Pallas kernels for 0%

profile of v1, /device:TPU:0, one launch (start us, length us, event | category | flops | bytes accessed | tf_op | source)
XLA Modules:
  0.0 445.6 jit_solution(593519723730391502)
XLA Ops:
  0.6 0.9 copy.12
  1.6 2.4 collective-permute-start.5
  4.0 1.0 fusion.39
  5.4 4.4 collective-permute-start.4
  9.8 40.7 %all-reduce.3 = (f32[32]{0:T(128)S(1)}, f32[32]{0:T(128)S(1)}) all-reduce(f32[32]{0:T(128)S(1)} %reduce_sum.73, f32[32]{0:T(128)S(1)} %reduce_sum.70), channel_id=1, replica_groups=mesh['tm'=16,'space'=2] {'tm','space'}, use_global_device_ids=true, to_apply=%region_5.0 | all-reduce | flops 64 | bytes 512 | tf_op jit(solution)/shard_map/psum | solution.py:45
  50.8 1.2 fusion.214
  52.0 39.8 %all-reduce.2 = (f32[256]{0:T(256)S(1)}, f32[256]{0:T(256)S(1)}) all-reduce(f32[256]{0:T(256)S(1)} %get-tuple-element.41, f32[256]{0:T(256)S(1)} %get-tuple-element.40), channel_id=1, replica_groups=mesh['tm'=16,'space'=2] {'tm','space'}, use_global_device_ids=true, to_apply=%region_10.11 | all-reduce | flops 512 | bytes 4096 | tf_op jit(solution)/shard_map/psum | solution.py:58
  91.8 0.7 fusion.217
  93.3 1.0 fusion.56
  94.3 1.0 copy.16
  95.3 1.1 reshape.522
  96.4 7.8 %all_to_all.15 = bf16[2,2,15360]{2,1,0:T(2,128)(2,1)S(1)} all-to-all(bf16[2,2,15360]{2,1,0:T(2,128)(2,1)S(1)} %reshape.522), channel_id=1, replica_groups=mesh['tm'=16,'space'=2] {'space'}, dimensions={0} | all-to-all | bytes 245760 | tf_op jit(solution)/shard_map/all_to_all | solution.py:72
  104.2 1.1 reshape.523
  105.3 0.8 copy.17
  106.2 10.9 %all_gather.3 = bf16[3,12,40,256]{3,1,0,2:T(8,128)(2,1)S(1)} all-gather(bf16[3,12,20,256]{3,1,0,2:T(8,128)(2,1)S(1)} %pad_maximum_fusion), channel_id=1, replica_groups=mesh['tm'=16,'space'=2] {'space'}, dimensions={2}, use_global_device_ids=true | all-gather | bytes 1105920 | tf_op jit(solution)/shard_map/all_gather | solution.py:71
  117.1 0.2 copy.15
  117.4 0.3 fusion.37
  117.6 0.3 fusion.36
  117.9 0.3 fusion.35
  118.2 0.3 fusion.34
  118.4 0.3 fusion.33
  118.7 0.3 fusion.32
  119.0 0.3 fusion.31
  119.2 0.3 fusion.30
  119.5 0.3 fusion.29
  119.8 0.3 fusion.28
  120.0 0.3 fusion.27
  120.3 0.3 fusion.26
  120.6 0.3 fusion.25
  120.8 0.3 fusion.24
  121.1 0.3 fusion.23
  121.4 0.3 fusion.22
  121.6 0.3 fusion.21
  121.9 0.3 fusion.20
  122.2 0.3 fusion.19
  122.4 0.3 fusion.18
  122.7 0.3 fusion.17
  123.0 0.3 fusion.16
  123.2 0.3 fusion.15
  123.5 0.3 fusion.14
  123.8 0.3 fusion.13
  124.0 0.3 fusion.12
  124.3 0.3 fusion.11
  124.6 6.2 %collective-permute-done.6 = f32[3,3,3,256,128]{4,3,2,1,0:T(8,128)S(1)} collective-permute-done((f32[3,3,3,256,128]{4,3,2,1,0:T(8,128)S(1)}, f32[3,3,3,256,128]{4,3,2,1,0:T(8,128)S(1)}, u32[]{:S(2)}, u32[]{:S(2)}) %collective-permute-start.6) | collective-permute-done | bytes 3538976 | tf_op jit(solution)/shard_map/ppermute | solution.py:112
  130.8 0.5 add.204
  131.4 1.5 collective-permute-start.7
  132.8 77.1 %collective-permute-done.7 = f32[3,3,3,256,128]{4,3,2,1,0:T(8,128)S(1)} collective-permute-done((f32[3,3,3,256,128]{4,3,2,1,0:T(8,128)S(1)}, f32[3,3,3,256,128]{4,3,2,1,0:T(8,128)S(1)}, u32[]{:S(2)}, u32[]{:S(2)}) %collective-permute-start.7) | collective-permute-done | bytes 3538976 | tf_op jit(solution)/shard_map/ppermute | solution.py:112
  210.0 0.5 add.205
  210.5 1.5 collective-permute-start.8
  212.0 2.2 collective-permute-start
  214.2 1.3 collective-permute-start.1
  216.2 3.6 collective-permute-done.1
  221.3 0.2 fusion.3
  222.0 66.2 %collective-permute-done.8 = f32[3,3,3,256,128]{4,3,2,1,0:T(8,128)S(1)} collective-permute-done((f32[3,3,3,256,128]{4,3,2,1,0:T(8,128)S(1)}, f32[3,3,3,256,128]{4,3,2,1,0:T(8,128)S(1)}, u32[]{:S(2)}, u32[]{:S(2)}) %collective-permute-start.8) | collective-permute-done | bytes 3538976 | tf_op jit(solution)/shard_map/ppermute | solution.py:112
  288.2 0.5 add.206
  288.7 2.2 collective-permute-start.9
  291.1 1.3 collective-permute-start.2
  292.9 0.2 fusion.1
  293.2 0.2 fusion
  293.9 1.3 collective-permute-start.3
  297.1 1.1 collective-permute-done.2
  298.2 0.7 add_convert_fusion
  298.9 144.5 %collective-permute-done.9 = f32[3,3,3,256,128]{4,3,2,1,0:T(8,128)S(1)} collective-permute-done((f32[3,3,3,256,128]{4,3,2,1,0:T(8,128)S(1)}, f32[3,3,3,256,128]{4,3,2,1,0:T(8,128)S(1)}, u32[]{:S(2)}, u32[]{:S(2)}) %collective-permute-start.9) | collective-permute-done | bytes 3538976 | tf_op jit(solution)/shard_map/ppermute | solution.py:112
  443.4 2.2 add.207
  (57 shorter events, 7.3 us)
Async XLA Ops:
  1.6 104.6 %collective-permute-start.5 = (bf16[1,12,20,256]{3,1,0,2:T(8,128)(2,1)S(1)}, bf16[1,12,20,256]{3,1,0,2:T(8,128)(2,1)S(1)}, u32[]{:S(2)}, u32[]{:S(2)}) collective-permute-start(bf16[1,12,20,256]{3,1,0,2:T(8,128)(2,1)S(1)} %copy.12), channel_id=1, source_target_pairs={{0,2},{2,4},{4,6},{6,8},{8,10},{10,12},{12,14},{14,16},{16,18},{18... | collective-permute-start | bytes 368648 | tf_op jit(solution)/shard_map/ppermute | solution.py:13
  5.4 100.8 %collective-permute-start.4 = (bf16[1,12,20,256]{3,1,0,2:T(8,128)(2,1)S(1)}, bf16[1,12,20,256]{3,1,0,2:T(8,128)(2,1)S(1)}, u32[]{:S(2)}, u32[]{:S(2)}) collective-permute-start(bf16[1,12,20,256]{3,1,0,2:T(8,128)(2,1)S(1)} %copy.12), channel_id=1, source_target_pairs={{0,4},{2,6},{4,8},{6,10},{8,12},{10,14},{12,16},{14,18},{16,20},{1... | collective-permute-start | bytes 368648 | tf_op jit(solution)/shard_map/ppermute | solution.py:13
  91.8 25.3 %copy-start.1 = (f32[256]{0:T(256)}, f32[256]{0:T(256)S(1)}, u32[]{:S(2)}) copy-start(f32[256]{0:T(256)S(1)} %get-tuple-element.44) | copy-start | bytes 3076
  91.8 25.3 %copy-start.2 = (f32[256]{0:T(256)}, f32[256]{0:T(256)S(1)}, u32[]{:S(2)}) copy-start(f32[256]{0:T(256)S(1)} %get-tuple-element.45) | copy-start | bytes 3076
  124.5 6.3 %collective-permute-start.6 = (f32[3,3,3,256,128]{4,3,2,1,0:T(8,128)S(1)}, f32[3,3,3,256,128]{4,3,2,1,0:T(8,128)S(1)}, u32[]{:S(2)}, u32[]{:S(2)}) collective-permute-start(f32[3,3,3,256,128]{4,3,2,1,0:T(8,128)S(1)} %bitcast.438), channel_id=1, source_target_pairs={{0,2},{2,0},{4,6},{6,4},{8,10},{10,8},{12,14},{14,12},{16,18},{18,... | collective-permute-start | bytes 10616840 | tf_op jit(solution)/shard_map/ppermute | solution.py:112
  131.3 84.2 %copy-start = (bf16[3,3,3,256,256]{4,3,2,1,0:T(8,128)(2,1)S(1)}, bf16[3,3,3,256,256]{4,3,2,1,0:T(8,128)(2,1)}, u32[]{:S(2)}) copy-start(bf16[3,3,3,256,256]{4,3,2,1,0:T(8,128)(2,1)} %param.14) | copy-start | bytes 10616836
  131.4 78.6 %collective-permute-start.7 = (f32[3,3,3,256,128]{4,3,2,1,0:T(8,128)S(1)}, f32[3,3,3,256,128]{4,3,2,1,0:T(8,128)S(1)}, u32[]{:S(2)}, u32[]{:S(2)}) collective-permute-start(f32[3,3,3,256,128]{4,3,2,1,0:T(8,128)S(1)} %add.204), channel_id=1, source_target_pairs={{0,4},{2,6},{4,0},{6,2},{8,12},{10,14},{12,8},{14,10},{16,20},{18,... | collective-permute-start | bytes 10616840 | tf_op jit(solution)/shard_map/ppermute | solution.py:112
  210.5 77.8 %collective-permute-start.8 = (f32[3,3,3,256,128]{4,3,2,1,0:T(8,128)S(1)}, f32[3,3,3,256,128]{4,3,2,1,0:T(8,128)S(1)}, u32[]{:S(2)}, u32[]{:S(2)}) collective-permute-start(f32[3,3,3,256,128]{4,3,2,1,0:T(8,128)S(1)} %add.205), channel_id=1, source_target_pairs={{0,8},{2,10},{4,12},{6,14},{8,0},{10,2},{12,4},{14,6},{16,24},{18,... | collective-permute-start | bytes 10616840 | tf_op jit(solution)/shard_map/ppermute | solution.py:112
  212.0 4.2 collective-permute-start
  214.2 5.6 %collective-permute-start.1 = (bf16[1,12,1,256]{3,2,1,0:T(2,128)(2,1)S(1)}, bf16[1,12,1,256]{3,2,1,0:T(2,128)(2,1)S(1)}, u32[]{:S(2)}, u32[]{:S(2)}) collective-permute-start(bf16[1,12,1,256]{3,2,1,0:T(2,128)(2,1)S(1)} %get-tuple-element.50), channel_id=1, source_target_pairs={{1,0},{3,2},{5,4},{7,6},{9,8},{11,10},{13,12},{15,14},{17,16},{19,... | collective-permute-start | bytes 18440 | tf_op jit(solution)/shard_map/ppermute | solution.py:26
  288.7 154.6 %collective-permute-start.9 = (f32[3,3,3,256,128]{4,3,2,1,0:T(8,128)S(1)}, f32[3,3,3,256,128]{4,3,2,1,0:T(8,128)S(1)}, u32[]{:S(2)}, u32[]{:S(2)}) collective-permute-start(f32[3,3,3,256,128]{4,3,2,1,0:T(8,128)S(1)} %add.206), channel_id=1, source_target_pairs={{0,16},{2,18},{4,20},{6,22},{8,24},{10,26},{12,28},{14,30},{16,0},... | collective-permute-start | bytes 10616840 | tf_op jit(solution)/shard_map/ppermute | solution.py:112
  291.1 7.0 %collective-permute-start.2 = (bf16[1,12,20,256]{3,2,1,0:T(8,128)(2,1)S(1)}, bf16[1,12,20,256]{3,2,1,0:T(8,128)(2,1)S(1)}, u32[]{:S(2)}, u32[]{:S(2)}) collective-permute-start(bf16[1,12,20,256]{3,2,1,0:T(8,128)(2,1)S(1)} %fusion.10), channel_id=1, source_target_pairs={{4,0},{6,2},{8,4},{10,6},{12,8},{14,10},{16,12},{18,14},{20,16},{2... | collective-permute-start | bytes 368648 | tf_op jit(solution)/shard_map/ppermute | solution.py:13
  293.9 4.3 collective-permute-start.3
